TPU v7x, 256 devices: a whole 4x4x8 slice. The times are simulated.
256 devices in a mesh: frame: 16 (over x, z_lo), fsdp: 16 (over z_hi, y, core).
Axes of the slice: x: 4, y: 4, z: 8 (z_hi: 2, z_lo: 4; z = z_hi * 4 + z_lo), core: 2. Of those that a mesh axis runs over, the one named last changes fastest.
Arguments:
- queries: bfloat16 [256, 192, 3072], P(('frame', 'fsdp')), may hold values from -18 to 18
- keys: bfloat16 [256, 192, 3072], P(('frame', 'fsdp')), may hold values from -7 to 7
- values: bfloat16 [256, 192, 3072], P(('frame', 'fsdp')), may hold values from -6 to 6
- residual: bfloat16 [256, 192, 3072], P(('frame', 'fsdp')), may hold values from -6 to 6
- target: bfloat16 [256, 192, 3072], P(('frame', 'fsdp')), may hold values from -6 to 6
- output_weight: bfloat16 [3072, 3072], P('fsdp'), may hold values from -0.109375 to 0.109375
- down_adapter: bfloat16 [16, 64, 3072], P('frame', None, 'fsdp'), may hold values from -0.109375 to 0.109375
- up_adapter: bfloat16 [16, 64, 3072], P('frame', None, 'fsdp'), may hold values from -1.1953125 to 1.1953125
- scene_of_frame: int32 [256], P(('frame', 'fsdp')), may hold values from 0 to 15
- scene_adapter_row: int32 [16], replicated, may hold values from 0 to 15, each once
- valid_token_count: int32 [256], P(('frame', 'fsdp')), may hold values from 1 to 192, 30720 in all
Outputs:
- grad_down: float32 [16, 64, 3072], P('frame', None, 'fsdp')
- grad_up: float32 [16, 64, 3072], P('frame', None, 'fsdp')
- frame_loss: float32 [256], P(('frame', 'fsdp'))
Inputs may be any that keep to these rules, and one draw needn't show every extreme that they name: `scene_adapter_row`: each scene has its own adapter row. `valid_token_count`: some frame has all 192 slots valid.
All inputs are finite; a program needn't handle non-finite values. No bound on the sum of `valid_token_count` on one device may be relied on, other than what follows from the above.
Results may differ from a plain program's by a relative error of at most 0.0053.
Values may be sent and summed in bfloat16 or wider, within the bound.
A program may use at most 192 MiB of HBM per device.

v0:
```python
import math
import jax
import jax.numpy as jnp
from jax import lax
from jax.sharding import PartitionSpec as P

HEADS = 24
adapter_scale = 2.0


def slot_lookup(scene_ids, scene_adapter_row):
    scene_range = jnp.arange(scene_adapter_row.shape[0], dtype=jnp.int32)
    matches = scene_ids[:, None] == scene_range[None, :]
    return jnp.sum(jnp.where(matches, scene_adapter_row[None, :], 0), axis=1)


def per_device(
    queries,
    keys,
    values,
    residual,
    target,
    output_weight,
    down_adapter,
    up_adapter,
    scene_of_frame,
    scene_adapter_row,
    valid_token_count,
):
    frames, slot_count, model_width = queries.shape
    head_count = HEADS
    head_size = model_width // head_count
    row_count = frames * slot_count
    score_scale = 1.0 / math.sqrt(head_size)
    query_heads = queries.reshape(frames, slot_count, head_count, head_size)
    key_heads = keys.reshape(frames, slot_count, head_count, head_size)
    value_heads = values.reshape(frames, slot_count, head_count, head_size)
    scores = (
        jnp.einsum("fqhd,fkhd->fhqk", query_heads, key_heads, preferred_element_type=jnp.float32)
        * score_scale
    )
    positions = lax.broadcasted_iota(jnp.int32, (frames, slot_count), 1)
    valid_mask = positions < valid_token_count[:, None]
    scores = jnp.where(valid_mask[:, None, None, :], scores, -jnp.inf)
    row_max = jnp.max(scores, axis=-1, keepdims=True)
    exponent = jnp.exp(scores - row_max)
    weights = (exponent / jnp.sum(exponent, axis=-1, keepdims=True)).astype(jnp.bfloat16)
    attended = jnp.einsum(
        "fhqk,fkhd->fqhd", weights, value_heads, preferred_element_type=jnp.float32
    )
    attended = attended.astype(jnp.bfloat16).reshape(frames, slot_count, model_width)
    mixed_flat = attended.reshape(row_count, model_width)
    projected_tokens = jnp.dot(
        mixed_flat,
        lax.all_gather(output_weight, "fsdp", axis=0, tiled=True),
        preferred_element_type=jnp.float32,
    )
    projected_tokens = projected_tokens.reshape(frames, slot_count, model_width)
    column_ids = lax.all_gather(scene_of_frame, "fsdp", axis=0, tiled=True)
    column_slots = slot_lookup(column_ids, scene_adapter_row)
    owner_range = jnp.arange(scene_adapter_row.shape[0], dtype=jnp.int32)
    column_pick = column_slots[:, None] == owner_range[None, :]
    adapter_couple = jnp.stack([down_adapter, up_adapter], axis=1)
    blocks = lax.all_gather(adapter_couple, "frame", axis=0, tiled=True)
    chosen = jnp.einsum(
        "fs,sxrd->fxrd",
        column_pick.astype(jnp.bfloat16),
        blocks,
        preferred_element_type=jnp.float32,
    )
    adapters = lax.all_to_all(
        chosen.astype(jnp.bfloat16), "fsdp", split_axis=0, concat_axis=3, tiled=True
    )
    down_weight_rows = adapters[:, 0]
    up_weight_rows = adapters[:, 1]
    low_rank_state = jnp.einsum(
        "ftd,frd->ftr", attended, down_weight_rows, preferred_element_type=jnp.float32
    ).astype(jnp.bfloat16)
    adapter_output = jnp.einsum(
        "akw,awe->ake", low_rank_state, up_weight_rows, preferred_element_type=jnp.float32
    )
    combined_output = (
        residual.astype(jnp.float32)
        + projected_tokens
        + adapter_scale * adapter_output
        - target.astype(jnp.float32)
    )
    residual_error = jnp.where(
        valid_mask[:, :, None], combined_output, jnp.zeros_like(combined_output)
    )
    token_float = valid_token_count.astype(jnp.float32)
    frame_loss = jnp.sum(residual_error * residual_error, axis=(1, 2)) / (token_float * model_width)
    output_gradient = (2.0 * residual_error / token_float[:, None, None]).astype(jnp.bfloat16)
    up_gradient_terms = adapter_scale * jnp.einsum(
        "ftr,ftd->frd", low_rank_state, output_gradient, preferred_element_type=jnp.float32
    )
    backward_low_rank = (
        adapter_scale
        * jnp.einsum(
            "ftd,frd->ftr", output_gradient, up_weight_rows, preferred_element_type=jnp.float32
        )
    ).astype(jnp.bfloat16)
    down_terms = jnp.einsum(
        "ftr,ftd->frd", backward_low_rank, attended, preferred_element_type=jnp.float32
    )
    grad_terms = jnp.stack([down_terms, up_gradient_terms], axis=1)
    pieces = lax.all_to_all(grad_terms, "fsdp", split_axis=3, concat_axis=0, tiled=True)
    scene_dense = jnp.einsum(
        "fs,fxrd->sxrd", column_pick.astype(jnp.float32), pieces, precision=lax.Precision.HIGHEST
    )
    scene_full = lax.psum(scene_dense, "frame")
    owned_rows = lax.dynamic_slice_in_dim(scene_full, lax.axis_index("frame"), 1, 0)
    return (owned_rows[:, 0], owned_rows[:, 1], frame_loss)


def solution(mesh):
    placed = (
        P(("frame", "fsdp"), None, None),
        P(("frame", "fsdp"), None, None),
        P(("frame", "fsdp"), None, None),
        P(("frame", "fsdp"), None, None),
        P(("frame", "fsdp"), None, None),
        P("fsdp", None),
        P("frame", None, "fsdp"),
        P("frame", None, "fsdp"),
        P(("frame", "fsdp")),
        P(),
        P(("frame", "fsdp")),
    )
    return jax.shard_map(
        per_device,
        mesh=mesh,
        in_specs=placed,
        out_specs=(P("frame", None, "fsdp"), P("frame", None, "fsdp"), P(("frame", "fsdp"))),
        check_vma=False,
    )
```

profile of v0, /device:TPU:16, one launch (start us, length us, event | category | flops | bytes accessed | tf_op | source)
XLA Modules:
  0.0 509.0 jit_solution(2743683499181057483)
XLA Ops:
  7.2 0.0 all-gather.2.cloned.1.call-start
  7.2 0.7 all-gather.2.cloned.1.call-update
  8.6 1.3 dynamic-slice
  9.8 0.8 dynamic-update-slice
  10.6 15.7 %all-reduce = s32[16]{0:T(128)S(1)} all-reduce(s32[16]{0:T(128)S(1)} %dynamic-update-slice), channel_id=1, replica_groups=mesh['frame'=16,'fsdp'=16] {'fsdp'}, use_global_device_ids=true, to_apply=%add | all-reduce | flops 16 | bytes 128
  26.3 0.8 select_reduce_fusion
  27.1 0.8 pad_maximum_fusion.1
  27.9 76.0 %all_gather.11 = bf16[16,2,64,192]{3,2,1,0:T(8,128)(2,1)S(1)} all-gather(bf16[1,2,64,192]{3,2,1,0:T(8,128)(2,1)S(1)} %pad_maximum_fusion.1), channel_id=1, replica_groups=mesh['frame'=16,'fsdp'=16] {'frame'}, dimensions={0}, use_global_device_ids=true | all-gather | bytes 835584 | tf_op jit(solution)/shard_map/all_gather | solution.py:64
  103.9 0.7 convolution_convert_fusion
  104.6 0.0 copy-start
  104.6 1.3 copy.63
  106.0 4.8 all-to-all-start
  110.8 0.0 all-reduce.3.cloned.1.call-start
  111.5 0.0 copy-done
  111.5 0.0 copy-start.1
  111.5 0.2 copy.74
  111.7 1.6 copy.75
  113.3 0.0 copy-done.1
  113.3 0.2 copy.76
  113.6 0.8 fusion.24
  114.4 2.0 fusion.51
  116.3 1.1 fusion.15
  117.5 1.8 copy.60
  119.3 54.0 %all-to-all-done = bf16[16,2,64,192]{3,2,1,0:T(8,128)(2,1)S(1)} async-done(((bf16[16,2,64,192]{3,2,1,0:T(8,128)(2,1)}), bf16[16,2,64,192]{3,2,1,0:T(8,128)(2,1)S(1)}, u32[]{:S(2)}, u32[]{:S(2)}) %all-to-all-start) | async-done | bytes 786464 | tf_op jit(solution)/shard_map/all_to_all | solution.py:71
  173.3 0.6 copy.64
  173.9 0.0 copy-start.2
  173.9 1.1 all_to_all.29
  175.0 1.8 fusion.33
  176.8 58.8 %all-gather.2.cloned.1.call-done = bf16[3072,3072]{1,0:T(8,128)(2,1)} async-done(((bf16[192,3072]{1,0:T(8,128)(2,1)}), bf16[3072,3072]{1,0:T(8,128)(2,1)}) %all-gather.2.cloned.1.call-update) | async-done | bytes 18874384 | tf_op jit(solution)/shard_map/all_gather | solution.py:55
  235.6 0.0 copy-done.2
  235.6 9.1 %fusion.5 = f32[1,192,3072]{2,1,0:T(8,128)S(1)} fusion(bf16[3072,3072]{1,0:T(8,128)(2,1)} %all-gather.2.cloned.1.call-done, bf16[1,192,3072]{2,1,0:T(8,128)(2,1)} %param.14, bf16[24,8,24,128]{3,2,1,0:T(8,128)(2,1)S(1)} %bitcast.107), kind=kOutput, calls=%fused_computation.10 | convolution fusion | flops 3625058304 | bytes 23592960 | tf_op jit(solution)/shard_map/dot_general | solution.py:53
  244.7 1.5 multiply_reduce_fusion
  246.2 1.3 fusion.7
  247.4 3.2 convolution_bitcast_fusion.1
  250.6 2.7 pad_maximum_fusion
  253.3 4.4 copy.65
  257.8 4.2 reshape.120
  262.0 42.7 %all_to_all.36 = f32[16,1,24576]{2,1,0:T(1,128)S(1)} all-to-all(f32[16,1,24576]{2,1,0:T(1,128)} %reshape.120), channel_id=1, replica_groups=mesh['frame'=16,'fsdp'=16] {'fsdp'}, dimensions={0} | all-to-all | bytes 3145728 | tf_op jit(solution)/shard_map/all_to_all | solution.py:107
  304.7 0.5 broadcast.46
  305.2 6.0 %reduce.5 = f32[16,24576]{1,0:T(8,128)} reduce(f32[16,1,24576]{2,1,0:T(1,128)S(1)} %all_to_all.36, f32[]{:T(128)} %broadcast.46), dimensions={1}, to_apply=%all_to_all.30.reduce_sub_computation | reduce | bytes 3145732 | tf_op jit(solution)/shard_map/all_to_all | solution.py:107
  311.2 3.4 reshape.121
  314.7 3.8 copy.73
  318.5 4.0 fusion.12
  322.5 0.0 all-reduce.3.cloned.1.call-update
  323.2 175.3 %all-reduce.3.cloned.1.call-done = f32[16,2,64,192]{3,0,2,1:T(8,128)} async-done(((f32[16,2,64,192]{3,0,2,1:T(8,128)}), f32[16,2,64,192]{3,0,2,1:T(8,128)}) %all-reduce.3.cloned.1.call-update) | async-done | bytes 1572880 | tf_op jit(solution)/shard_map/psum | solution.py:111
  498.5 1.3 dynamic-slice_bitcast_fusion
  499.8 0.6 copy.67
  500.4 0.6 copy.68
  (4 shorter events, 0.0 us)
Async XLA Ops:
  7.2 228.4 %all-gather.2.cloned.1.call-start = ((), (), s32[]{:S(2)}) async-start(), calls=%async_computation.2 | async-start | bytes 20054016 | tf_op jit(solution)/shard_map/all_gather | solution.py:55
  104.6 6.9 %copy-start = (bf16[1,192,3072]{2,1,0:T(8,128)(2,1)S(1)}, bf16[1,192,3072]{2,1,0:T(8,128)(2,1)}, u32[]{:S(2)}) copy-start(bf16[1,192,3072]{2,1,0:T(8,128)(2,1)} %param.11) | copy-start | bytes 3538948
  106.0 67.3 %all-to-all-start = ((bf16[16,2,64,192]{3,2,1,0:T(8,128)(2,1)}), bf16[16,2,64,192]{3,2,1,0:T(8,128)(2,1)S(1)}, u32[]{:S(2)}, u32[]{:S(2)}) async-start(bf16[16,2,64,192]{3,2,1,0:T(8,128)(2,1)} %copy.63), calls=%async_computation | async-start | bytes 2097152 | tf_op jit(solution)/shard_map/all_to_all | solution.py:71
  110.8 387.7 %all-reduce.3.cloned.1.call-start = ((), (), s32[]{:S(2)}) async-start(), calls=%async_computation.3 | async-start | bytes 4194304 | tf_op jit(solution)/shard_map/psum | solution.py:111
  111.5 1.8 copy-start.1
  173.9 61.7 %copy-start.2 = (bf16[1,192,24,128]{3,2,1,0:T(8,128)(2,1)S(1)}, bf16[1,192,24,128]{3,2,1,0:T(8,128)(2,1)}, u32[]{:S(2)}) copy-start(bf16[1,192,24,128]{3,2,1,0:T(8,128)(2,1)} %copy.60) | copy-start | bytes 3538948
  235.6 9.1 %copy-start.3 = (bf16[1,192,3072]{2,1,0:T(8,128)(2,1)S(1)}, bf16[1,192,3072]{2,1,0:T(8,128)(2,1)}, u32[]{:S(2)}) copy-start(bf16[1,192,3072]{2,1,0:T(8,128)(2,1)} %param.15) | copy-start | bytes 3538948
Sparse Core Ops, SparseCore 0:
  10.7 224.8 all-gather.1
  322.6 175.7 all-reduce.2
where the time goes:
time: 510 us; the launch traced here: 509 us
  waiting for transfers between devices  289 us (57%)
  blocking collectives  134 us (26%)
  local copies, waits for them, and re-layouts  27.8 us (5%)
  matrix products  23.4 us (5%)
  between operations  17.3 us (3%)
  other arithmetic  12.3 us (2%)
    psum x1, waiting for transfers between devices, per_device(): scene_full = lax.psum(scene_dense, 'frame')  175 us
    all_gather x1, blocking collectives, per_device(): blocks = lax.all_gather(adapter_couple, 'frame', axis=0, tiled=True)  76 us
    all_gather x1, waiting for transfers between devices, per_device(): lax.all_gather(output_weight, 'fsdp', axis=0, tiled=True)  58.8 us
    all_to_all x1, waiting for transfers between devices, per_device(): lax.all_to_all(chosen.astype(jnp.bfloat16), 'fsdp', split_axis=0, concat_...  54 us
    all_to_all x1, blocking collectives, per_device(): lax.all_to_all(grad_terms, 'fsdp', split_axis=3, concat_axis=0, tiled=True)  42.7 us
    unnamed x1, blocking collectives  15.7 us
    unnamed x18, local copies, waits for them, and re-layouts  13 us
  transfers between devices with their start and end apart: 3, of which 3 were waited for; matrix products, arithmetic and copies ran while one was open for 3% of the time, Pallas kernels for 0%

commit v1 on v0

--- a/solution.py
+++ b/solution.py
@@ -3,6 +3,7 @@
 import jax.numpy as jnp
 from jax import lax
 from jax.sharding import PartitionSpec as P
+from jax.lax import all_to_all, axis_size
 
 HEADS = 24
 adapter_scale = 2.0
@@ -61,7 +62,14 @@
     owner_range = jnp.arange(scene_adapter_row.shape[0], dtype=jnp.int32)
     column_pick = column_slots[:, None] == owner_range[None, :]
     adapter_couple = jnp.stack([down_adapter, up_adapter], axis=1)
-    blocks = lax.all_gather(adapter_couple, "frame", axis=0, tiled=True)
+
+    def guide_node(buf, where_dim):
+        front = jnp.concatenate(
+            all_to_all(jnp.stack([buf] * axis_size("frame"), 0), "frame", 0, 0), where_dim
+        )
+        return front
+
+    blocks = guide_node(adapter_couple, 0)
     chosen = jnp.einsum(
         "fs,sxrd->fxrd",
         column_pick.astype(jnp.bfloat16),

time: 510 us -> 505 us (level)
  blocking collectives: 134 us -> 72.4 us
  waiting for transfers between devices: 289 us -> 335 us
  starting transfers between devices: 4.89 us -> 17.3 us
    all_gather x1 -> x0, blocking collectives: 76 us -> none  [per_device(): blocks = lax.all_gather(adapter_couple, 'frame', axis=0, tiled=True)]
    all_to_all x1, waiting for transfers between devices: 54 us -> 80.8 us  [per_device(): lax.all_to_all(chosen.astype(jnp.bfloat16), 'fsdp', split_axis=0, concat_...]
    all_to_all x0 -> x1, waiting for transfers between devices: none -> 20.4 us  [guide_node(): all_to_all(jnp.stack([buf] * axis_size('frame'), 0), 'frame', 0, 0)]
    unnamed x1, blocking collectives: 15.7 us -> 27.2 us
    all_to_all x0 -> x1, starting transfers between devices: none -> 8.47 us  [guide_node(): all_to_all(jnp.stack([buf] * axis_size('frame'), 0), 'frame', 0, 0)]
    unnamed x18 -> x26, local copies, waits for them, and re-layouts: 13 us -> 12.9 us
  transfers between devices with their start and end apart: 3 -> 4, of which waited for: 3 -> 4; matrix products, arithmetic and copies ran while one was open for 3% -> 3% of each run, Pallas kernels for 0% -> 0%
where the time goes in v1:
time: 505 us; the launch traced here: 504 us
  waiting for transfers between devices  335 us (66%)
  blocking collectives  72.4 us (14%)
  local copies, waits for them, and re-layouts  27.8 us (6%)
  matrix products  22.2 us (4%)
  between operations  17.4 us (3%)
  starting transfers between devices  17.3 us (3%)
  other arithmetic  11.7 us (2%)
    psum x1, waiting for transfers between devices, per_device(): scene_full = lax.psum(scene_dense, 'frame')  175 us
    all_to_all x1, waiting for transfers between devices, per_device(): lax.all_to_all(chosen.astype(jnp.bfloat16), 'fsdp', split_axis=0, concat_...  80.8 us
    all_gather x1, waiting for transfers between devices, per_device(): lax.all_gather(output_weight, 'fsdp', axis=0, tiled=True)  58.5 us
    all_to_all x1, blocking collectives, per_device(): lax.all_to_all(grad_terms, 'fsdp', split_axis=3, concat_axis=0, tiled=True)  45.2 us
    unnamed x1, blocking collectives  27.2 us
    all_to_all x1, waiting for transfers between devices, guide_node(): all_to_all(jnp.stack([buf] * axis_size('frame'), 0), 'frame', 0, 0)  20.4 us
    unnamed x26, local copies, waits for them, and re-layouts  12.9 us
  transfers between devices with their start and end apart: 4, of which 4 were waited for; matrix products, arithmetic and copies ran while one was open for 3% of the time, Pallas kernels for 0%

profile of v1, /device:TPU:16, one launch (start us, length us, event | category | flops | bytes accessed | tf_op | source)
XLA Modules:
  0.0 504.1 jit_solution(8600168553382813680)
XLA Ops:
  7.2 0.0 all-gather.2.cloned.1.call-start
  7.2 0.7 all-gather.2.cloned.1.call-update
  7.9 0.8 maximum_bitcast_fusion
  8.7 1.1 stack.20
  9.8 8.5 %all-to-all-start = ((bf16[16,1,2,64,192]{4,3,2,1,0:T(8,128)(2,1)}), bf16[16,1,2,64,192]{4,3,2,1,0:T(8,128)(2,1)S(1)}, u32[]{:S(2)}, u32[]{:S(2)}) async-start(bf16[16,1,2,64,192]{4,3,2,1,0:T(8,128)(2,1)} %stack.20), calls=%async_computation | async-start | bytes 2097152 | tf_op jit(solution)/shard_map/all_to_all | solution.py:68
  18.3 0.0 copy-start.1
  19.0 0.0 copy-start.2
  19.1 0.2 copy.72
  19.3 0.3 copy-done.1
  19.6 0.2 copy.73
  19.8 0.6 copy-done.2
  20.4 1.3 copy.74
  22.4 0.6 dynamic-slice
  22.9 0.8 dynamic-update-slice
  23.7 27.2 %all-reduce = s32[16]{0:T(128)S(1)} all-reduce(s32[16]{0:T(128)S(1)} %dynamic-update-slice), channel_id=1, replica_groups=mesh['frame'=16,'fsdp'=16] {'fsdp'}, use_global_device_ids=true, to_apply=%add | all-reduce | flops 16 | bytes 128
  50.9 0.2 select_reduce_fusion
  51.1 20.4 %all-to-all-done = bf16[16,1,2,64,192]{4,3,2,1,0:T(8,128)(2,1)S(1)} async-done(((bf16[16,1,2,64,192]{4,3,2,1,0:T(8,128)(2,1)}), bf16[16,1,2,64,192]{4,3,2,1,0:T(8,128)(2,1)S(1)}, u32[]{:S(2)}, u32[]{:S(2)}) %all-to-all-start) | async-done | bytes 786464 | tf_op jit(solution)/shard_map/all_to_all | solution.py:68
  71.5 0.7 convolution_convert_fusion
  72.2 1.3 copy.61
  73.6 8.8 %all-to-all-start.1 = ((bf16[16,2,64,192]{3,2,1,0:T(8,128)(2,1)}), bf16[16,2,64,192]{3,2,1,0:T(8,128)(2,1)S(1)}, u32[]{:S(2)}, u32[]{:S(2)}) async-start(bf16[16,2,64,192]{3,2,1,0:T(8,128)(2,1)} %copy.61), calls=%async_computation.1 | async-start | bytes 2097152 | tf_op jit(solution)/shard_map/all_to_all | solution.py:79
  82.3 0.0 all-reduce.3.cloned.1.call-start
  82.4 0.8 fusion.24
  83.2 2.0 fusion.52
  85.2 1.1 fusion.15
  86.3 0.8 copy.58
  87.1 80.8 %all-to-all-done.1 = bf16[16,2,64,192]{3,2,1,0:T(8,128)(2,1)S(1)} async-done(((bf16[16,2,64,192]{3,2,1,0:T(8,128)(2,1)}), bf16[16,2,64,192]{3,2,1,0:T(8,128)(2,1)S(1)}, u32[]{:S(2)}, u32[]{:S(2)}) %all-to-all-start.1) | async-done | bytes 786464 | tf_op jit(solution)/shard_map/all_to_all | solution.py:79
  167.8 0.6 copy.62
  168.4 1.1 all_to_all.33
  169.6 0.5 fusion.33
  170.1 58.5 %all-gather.2.cloned.1.call-done = bf16[3072,3072]{1,0:T(8,128)(2,1)} async-done(((bf16[192,3072]{1,0:T(8,128)(2,1)}), bf16[3072,3072]{1,0:T(8,128)(2,1)}) %all-gather.2.cloned.1.call-update) | async-done | bytes 18874384 | tf_op jit(solution)/shard_map/all_gather | solution.py:56
  228.6 9.1 %fusion.5 = f32[1,192,3072]{2,1,0:T(8,128)S(1)} fusion(bf16[3072,3072]{1,0:T(8,128)(2,1)} %all-gather.2.cloned.1.call-done, bf16[1,192,3072]{2,1,0:T(8,128)(2,1)} %param.14, bf16[24,8,24,128]{3,2,1,0:T(8,128)(2,1)S(1)} %bitcast.112), kind=kOutput, calls=%fused_computation.10 | convolution fusion | flops 3625058304 | bytes 23592960 | tf_op jit(solution)/shard_map/dot_general | solution.py:54
  237.7 1.5 multiply_reduce_fusion
  239.1 1.3 fusion.7
  240.4 3.2 convolution_bitcast_fusion.1
  243.6 2.7 pad_maximum_fusion
  246.3 4.4 copy.63
  250.7 4.2 reshape.127
  255.0 45.2 %all_to_all.41 = f32[16,1,24576]{2,1,0:T(1,128)S(1)} all-to-all(f32[16,1,24576]{2,1,0:T(1,128)} %reshape.127), channel_id=1, replica_groups=mesh['frame'=16,'fsdp'=16] {'fsdp'}, dimensions={0} | all-to-all | bytes 3145728 | tf_op jit(solution)/shard_map/all_to_all | solution.py:115
  300.1 0.5 broadcast.49
  300.7 6.0 %reduce.5 = f32[16,24576]{1,0:T(8,128)} reduce(f32[16,1,24576]{2,1,0:T(1,128)S(1)} %all_to_all.41, f32[]{:T(128)} %broadcast.49), dimensions={1}, to_apply=%all_to_all.34.reduce_sub_computation | reduce | bytes 3145732 | tf_op jit(solution)/shard_map/all_to_all | solution.py:115
  306.7 3.4 reshape.128
  310.1 3.8 copy.71
  313.9 4.0 fusion.12
  317.9 0.0 all-reduce.3.cloned.1.call-update
  318.6 175.0 %all-reduce.3.cloned.1.call-done = f32[16,2,64,192]{3,0,2,1:T(8,128)} async-done(((f32[16,2,64,192]{3,0,2,1:T(8,128)}), f32[16,2,64,192]{3,0,2,1:T(8,128)}) %all-reduce.3.cloned.1.call-update) | async-done | bytes 1572880 | tf_op jit(solution)/shard_map/psum | solution.py:119
  493.6 1.3 dynamic-slice_bitcast_fusion
  494.9 0.6 copy.65
  495.5 0.6 copy.66
  (14 shorter events, 0.0 us)
Async XLA Ops:
  7.2 11.9 %copy-start = (bf16[1,192,3072]{2,1,0:T(8,128)(2,1)S(1)}, bf16[1,192,3072]{2,1,0:T(8,128)(2,1)}, u32[]{:S(2)}) copy-start(bf16[1,192,3072]{2,1,0:T(8,128)(2,1)} %param.11) | copy-start | bytes 3538948
  7.2 221.4 %all-gather.2.cloned.1.call-start = ((), (), s32[]{:S(2)}) async-start(), calls=%async_computation.3 | async-start | bytes 20054016 | tf_op jit(solution)/shard_map/all_gather | solution.py:56
  9.8 61.7 %all-to-all-start = ((bf16[16,1,2,64,192]{4,3,2,1,0:T(8,128)(2,1)}), bf16[16,1,2,64,192]{4,3,2,1,0:T(8,128)(2,1)S(1)}, u32[]{:S(2)}, u32[]{:S(2)}) async-start(bf16[16,1,2,64,192]{4,3,2,1,0:T(8,128)(2,1)} %stack.20), calls=%async_computation | async-start | bytes 2097152 | tf_op jit(solution)/shard_map/all_to_all | solution.py:68
  18.3 1.3 copy-start.1
  19.0 1.4 copy-start.2
  19.6 2.8 copy-start.7
  19.6 31.3 %copy-start.6 = (s32[16]{0:T(128)S(1)}, s32[16]{0:T(128)}, u32[]{:S(2)}) copy-start(s32[16]{0:T(128)} %param.20) | copy-start | bytes 196
  73.6 94.3 %all-to-all-start.1 = ((bf16[16,2,64,192]{3,2,1,0:T(8,128)(2,1)}), bf16[16,2,64,192]{3,2,1,0:T(8,128)(2,1)S(1)}, u32[]{:S(2)}, u32[]{:S(2)}) async-start(bf16[16,2,64,192]{3,2,1,0:T(8,128)(2,1)} %copy.61), calls=%async_computation.1 | async-start | bytes 2097152 | tf_op jit(solution)/shard_map/all_to_all | solution.py:79
  82.3 411.3 %all-reduce.3.cloned.1.call-start = ((), (), s32[]{:S(2)}) async-start(), calls=%async_computation.4 | async-start | bytes 4194304 | tf_op jit(solution)/shard_map/psum | solution.py:119
  83.2 2.0 copy-start.3
  87.1 141.5 %copy-start.4 = (bf16[1,192,24,128]{3,2,1,0:T(8,128)(2,1)}, bf16[1,192,24,128]{3,2,1,0:T(8,128)(2,1)S(1)}, u32[]{:S(2)}) copy-start(bf16[1,192,24,128]{3,2,1,0:T(8,128)(2,1)S(1)} %copy.58) | copy-start | bytes 3538948
  228.6 9.1 %copy-start.5 = (bf16[1,192,3072]{2,1,0:T(8,128)(2,1)S(1)}, bf16[1,192,3072]{2,1,0:T(8,128)(2,1)}, u32[]{:S(2)}) copy-start(bf16[1,192,3072]{2,1,0:T(8,128)(2,1)} %param.15) | copy-start | bytes 3538948
Sparse Core Ops, SparseCore 0:
  10.7 217.8 all-gather.1
  318.1 175.5 all-reduce.2
